TPU v7x, 32 devices: a whole 2x2x4 slice. The times are simulated.
32 devices in a mesh: wide: 8 (over y, x, core), narrow: 4 (over z).
Axes of the slice: x: 2, y: 2, z: 4, core: 2. Of those that a mesh axis runs over, the one named last changes fastest.
Arguments:
- states: bfloat16 [16384, 1024], P(('wide', 'narrow')), may hold values from -6 to 6
- applied: bfloat16 [16384, 1024], P(('wide', 'narrow')), may hold values from -6 to 6
- rotation: bfloat16 [2, 1024, 256], P(None, 'wide', 'narrow'), may hold values from -0.1875 to 0.1875
- ritz: float32 [2, 256], replicated, may hold values from 0.5 to 4
- potential: float32 [16384], P(('wide', 'narrow')), may hold values from 0.5 to 8
Outputs:
- rotated: bfloat16 [16384, 2, 256], P(('wide', 'narrow'))
- correction: bfloat16 [16384, 2, 256], P(('wide', 'narrow'))
- margin: float32 [2, 1024, 256], P(None, 'wide', 'narrow')
All inputs are finite; a program needn't handle non-finite values.
Results may differ from a plain program's by a relative error of at most 0.0095.
Values may be sent and summed in bfloat16 or wider, within the bound.
A program may use at most 64 MiB of HBM per device.

v0:
```python
import math
import jax
import jax.numpy as jnp
from jax import lax
from jax.sharding import PartitionSpec as P


def per_device(states, applied, rotation, ritz, potential):
    row_count = states.shape[0]
    total_rows = row_count * lax.axis_size("wide") * lax.axis_size("narrow")
    factor = 1.0 / math.sqrt(total_rows)
    contract = (((0,), (0,)), ((), ()))
    rotated_list = []
    correction_list = []
    margin_list = []
    for window in range(rotation.shape[0]):
        q_local = rotation[window]
        q_tall = lax.all_gather(q_local, "wide", axis=0, tiled=True)
        q_full = lax.all_gather(q_tall, "narrow", axis=1, tiled=True)
        plain = jnp.dot(states, q_full, preferred_element_type=jnp.float32)
        mapped = jnp.dot(applied, q_full, preferred_element_type=jnp.float32)
        eigen_values = ritz[window]
        residual = mapped - plain * eigen_values[None, :]
        fixed = (residual / (potential[:, None] + eigen_values[None, :])).astype(jnp.bfloat16)
        partial_value = lax.psum_scatter(
            lax.dot_general(states, fixed, contract, preferred_element_type=jnp.float32).astype(
                jnp.bfloat16
            ),
            "wide",
            scatter_dimension=0,
            tiled=True,
        )
        summed = lax.psum_scatter(partial_value, "narrow", scatter_dimension=1, tiled=True).astype(
            jnp.float32
        )
        rotated_list.append(plain.astype(jnp.bfloat16))
        correction_list.append(fixed)
        margin_list.append(summed * factor)
    return (
        jnp.stack(rotated_list, axis=1),
        jnp.stack(correction_list, axis=1),
        jnp.stack(margin_list, axis=0),
    )


def solution(mesh):
    placed = (
        P(("wide", "narrow"), None),
        P(("wide", "narrow"), None),
        P(None, "wide", "narrow"),
        P(),
        P(("wide", "narrow")),
    )
    return jax.shard_map(
        per_device,
        mesh=mesh,
        in_specs=placed,
        out_specs=(
            P(("wide", "narrow"), None, None),
            P(("wide", "narrow"), None, None),
            P(None, "wide", "narrow"),
        ),
        check_vma=False,
    )
```

profile of v0, /device:TPU:0, one launch (start us, length us, event | category | flops | bytes accessed | tf_op | source)
XLA Modules:
  0.0 160.5 jit_solution(8119105058409660867)
XLA Ops:
  7.2 0.0 copy-start
  7.2 0.0 reduce-scatter.15.cloned.1.call-start
  7.2 0.8 fusion.13
  8.0 0.7 fusion.12
  8.7 10.5 %all-gather.2 = bf16[1,1024,64]{1,2,0:T(8,128)(2,1)S(1)} all-gather(bf16[1,128,64]{1,2,0:T(8,128)(2,1)S(1)} %get-tuple-element.10), channel_id=4, replica_groups=mesh['wide'=8,'narrow'=4] {'wide'}, dimensions={1}, use_global_device_ids=true | all-gather | bytes 147456 | tf_op jit(solution)/shard_map/all_gather | solution.py:18
  19.3 16.3 %all-gather.3 = bf16[1,1024,256]{1,2,0:T(8,128)(2,1)S(1)} all-gather(bf16[1,1024,64]{1,2,0:T(8,128)(2,1)S(1)} %all-gather.2), channel_id=5, replica_groups=mesh['wide'=8,'narrow'=4] {'narrow'}, dimensions={2}, use_global_device_ids=true | all-gather | bytes 655360 | tf_op jit(solution)/shard_map/all_gather | solution.py:19
  35.6 0.0 copy-done
  35.6 0.0 copy-start.1
  35.6 0.5 fusion.7
  36.1 0.0 copy-start.3
  36.1 0.7 copy-done.1
  36.8 0.0 copy-done.3
  36.8 0.5 fusion.4
  37.3 0.5 fusion.3
  37.8 1.0 copy.14
  38.8 0.0 reduce-scatter.15.cloned.1.call-update
  38.8 0.0 reduce-scatter.13.cloned.1.call-start
  38.9 9.0 %all-gather = bf16[1,1024,64]{1,2,0:T(8,128)(2,1)S(1)} all-gather(bf16[1,128,64]{1,2,0:T(8,128)(2,1)S(1)} %get-tuple-element.9), channel_id=2, replica_groups=mesh['wide'=8,'narrow'=4] {'wide'}, dimensions={1}, use_global_device_ids=true | all-gather | bytes 147456 | tf_op jit(solution)/shard_map/all_gather | solution.py:18
  47.9 16.6 %all-gather.1 = bf16[1,1024,256]{1,2,0:T(8,128)(2,1)S(1)} all-gather(bf16[1,1024,64]{1,2,0:T(8,128)(2,1)S(1)} %all-gather), channel_id=3, replica_groups=mesh['wide'=8,'narrow'=4] {'narrow'}, dimensions={2}, use_global_device_ids=true | all-gather | bytes 655360 | tf_op jit(solution)/shard_map/all_gather | solution.py:19
  64.5 0.0 copy-start.2
  64.5 0.5 fusion.10
  65.0 0.7 copy-done.2
  65.7 0.5 fusion.5
  66.2 0.5 fusion.2
  66.6 1.0 copy.12
  67.6 0.0 reduce-scatter.13.cloned.1.call-update
  67.7 0.0 reduce-scatter.11.cloned.1.call-start
  67.8 5.8 %reduce-scatter.15.cloned.1.call-done = bf16[128,256]{1,0:T(8,128)(2,1)} async-done(((bf16[1024,256]{1,0:T(8,128)(2,1)}), bf16[128,256]{1,0:T(8,128)(2,1)}) %reduce-scatter.15.cloned.1.call-update) | async-done | bytes 65552
  73.6 1.6 copy.15
  75.2 0.0 reduce-scatter.11.cloned.1.call-update
  75.2 0.0 reduce-scatter.9.cloned.1.call-start
  75.3 0.1 pad_maximum_fusion
  75.3 1.3 copy.10
  76.7 0.1 pad_maximum_fusion.1
  76.7 1.3 copy.11
  78.0 32.8 %reduce-scatter.13.cloned.1.call-done = bf16[128,256]{1,0:T(8,128)(2,1)} async-done(((bf16[1024,256]{1,0:T(8,128)(2,1)}), bf16[128,256]{1,0:T(8,128)(2,1)}) %reduce-scatter.13.cloned.1.call-update) | async-done | bytes 65552
  110.9 1.6 copy.13
  112.4 0.0 reduce-scatter.9.cloned.1.call-update
  112.5 20.6 %reduce-scatter.11.cloned.1.call-done = bf16[128,64]{0,1:T(8,128)(2,1)} async-done(((bf16[128,256]{0,1:T(8,128)(2,1)}), bf16[128,64]{0,1:T(8,128)(2,1)}) %reduce-scatter.11.cloned.1.call-update) | async-done | bytes 16400 | tf_op jit(solution)/shard_map/reduce_scatter | solution.py:33
  133.0 0.7 multiply_bitcast_fusion
  133.7 18.9 %reduce-scatter.9.cloned.1.call-done = bf16[128,64]{0,1:T(8,128)(2,1)} async-done(((bf16[128,256]{0,1:T(8,128)(2,1)}), bf16[128,64]{0,1:T(8,128)(2,1)}) %reduce-scatter.9.cloned.1.call-update) | async-done | bytes 16400 | tf_op jit(solution)/shard_map/reduce_scatter | solution.py:33
  152.6 0.7 multiply_bitcast_fusion.1
  153.3 0.6 pad_maximum_fusion.2
  (2 shorter events, 0.1 us)
Async XLA Ops:
  7.2 28.4 %copy-start = (bf16[512,1024]{1,0:T(8,128)(2,1)S(1)}, bf16[512,1024]{1,0:T(8,128)(2,1)}, u32[]{:S(2)}) copy-start(bf16[512,1024]{1,0:T(8,128)(2,1)} %param.5) | copy-start | bytes 3145732
  7.2 66.4 %reduce-scatter.15.cloned.1.call-start = ((), (), s32[]{:S(2)}) async-start(), calls=%async_computation.7 | async-start | bytes 589824
  35.6 1.2 copy-start.1
  36.1 0.7 copy-start.3
  38.8 72.1 %reduce-scatter.13.cloned.1.call-start = ((), (), s32[]{:S(2)}) async-start(), calls=%async_computation.6 | async-start | bytes 589824
  64.5 1.2 copy-start.2
  67.7 65.3 %reduce-scatter.11.cloned.1.call-start = ((), (), s32[]{:S(2)}) async-start(), calls=%async_computation.5 | async-start | bytes 81920 | tf_op jit(solution)/shard_map/reduce_scatter | solution.py:33
  75.2 77.4 %reduce-scatter.9.cloned.1.call-start = ((), (), s32[]{:S(2)}) async-start(), calls=%async_computation.4 | async-start | bytes 81920 | tf_op jit(solution)/shard_map/reduce_scatter | solution.py:33
Sparse Core Ops, SparseCore 0:
  38.9 34.6 reduce-scatter.14
  76.7 34.1 reduce-scatter.12
  113.7 19.2 reduce-scatter.10
  135.1 17.4 reduce-scatter.8
where the time goes:
time: 161 us; the launch traced here: 160 us
  waiting for transfers between devices  78.1 us (49%)
  blocking collectives  52.5 us (33%)
  between operations  13.9 us (9%)
  local copies, waits for them, and re-layouts  10.8 us (7%)
  matrix products  2.82 us (2%)
  other arithmetic  2.24 us (1%)
    reduce_scatter x2, waiting for transfers between devices, per_device(): lax.psum_scatter(partial_value, 'narrow', scatter_dimension=1, tiled=True)  39.4 us
    unnamed x6, waiting for transfers between devices  38.7 us
    all_gather x2, blocking collectives, per_device(): q_full = lax.all_gather(q_tall, 'narrow', axis=1, tiled=True)  32.9 us
    all_gather x2, blocking collectives, per_device(): q_tall = lax.all_gather(q_local, 'wide', axis=0, tiled=True)  19.6 us
    unnamed x14, local copies, waits for them, and re-layouts  9.3 us
  transfers between devices with their start and end apart: 4, of which 4 were waited for; matrix products, arithmetic and copies ran while one was open for 6% of the time, Pallas kernels for 0%

commit v1 on v0

--- a/solution.py
+++ b/solution.py
@@ -3,6 +3,24 @@
 import jax.numpy as jnp
 from jax import lax
 from jax.sharding import PartitionSpec as P
+
+
+def collect(shard, axis, dim):
+    ways, here, step = (lax.axis_size(axis), lax.axis_index(axis), shard.shape[dim])
+    dims = [n * ways if d == dim else n for d, n in enumerate(shard.shape)]
+    full = lax.dynamic_update_slice_in_dim(
+        jnp.zeros(dims, shard.dtype), shard, here * step, axis=dim
+    )
+    going_up = going_down = shard
+    for far in range(1, ways // 2 + 1):
+        going_up = lax.ppermute(going_up, axis, [(d, (d + 1) % ways) for d in range(ways)])
+        full = lax.dynamic_update_slice_in_dim(full, going_up, (here - far) % ways * step, axis=dim)
+        if 2 * far < ways:
+            going_down = lax.ppermute(going_down, axis, [(d, (d - 1) % ways) for d in range(ways)])
+            full = lax.dynamic_update_slice_in_dim(
+                full, going_down, (here + far) % ways * step, axis=dim
+            )
+    return full
 
 
 def per_device(states, applied, rotation, ritz, potential):
@@ -15,7 +33,7 @@
     margin_list = []
     for window in range(rotation.shape[0]):
         q_local = rotation[window]
-        q_tall = lax.all_gather(q_local, "wide", axis=0, tiled=True)
+        q_tall = collect(q_local, "wide", 0)
         q_full = lax.all_gather(q_tall, "narrow", axis=1, tiled=True)
         plain = jnp.dot(states, q_full, preferred_element_type=jnp.float32)
         mapped = jnp.dot(applied, q_full, preferred_element_type=jnp.float32)

time: 161 us -> 187 us (1.16)
  waiting for transfers between devices: 78.1 us -> 105 us
  blocking collectives: 52.5 us -> 33.2 us
  starting transfers between devices: 0.16 us -> 16.8 us
    unnamed x6, waiting for transfers between devices: 38.7 us -> 61.6 us
    all_gather x2 -> x0, blocking collectives: 19.6 us -> none  [per_device(): q_tall = lax.all_gather(q_local, 'wide', axis=0, tiled=True)]
    ppermute x0 -> x14, starting transfers between devices: none -> 16.7 us  [the longest x6 16.1 us: collect(): lax.ppermute(going_down, axis, [(d, (d - 1) % ways) for d in range(ways)])]
    ppermute x0 -> x14, waiting for transfers between devices: none -> 3.99 us  [the longest x8 3.97 us: collect(): lax.ppermute(going_up, axis, [(d, (d + 1) % ways) for d in range(ways)])]
    unnamed x14 -> x22, local copies, waits for them, and re-layouts: 9.3 us -> 10.9 us
  transfers between devices with their start and end apart: 4 -> 18, of which waited for: 4 -> 6; matrix products, arithmetic and copies ran while one was open for 6% -> 5% of each run, Pallas kernels for 0% -> 0%
where the time goes in v1:
time: 187 us; the launch traced here: 186 us
  waiting for transfers between devices  105 us (56%)
  blocking collectives  33.2 us (18%)
  starting transfers between devices  16.8 us (9%)
  between operations  14 us (7%)
  local copies, waits for them, and re-layouts  12 us (6%)
  matrix products  2.8 us (1%)
  other arithmetic  2.25 us (1%)
    unnamed x6, waiting for transfers between devices  61.6 us
    reduce_scatter x2, waiting for transfers between devices, per_device(): lax.psum_scatter(partial_value, 'narrow', scatter_dimension=1, tiled=True)  39.3 us
    all_gather x2, blocking collectives, per_device(): q_full = lax.all_gather(q_tall, 'narrow', axis=1, tiled=True)  33.2 us
    ppermute x6, starting transfers between devices, collect(): lax.ppermute(going_down, axis, [(d, (d - 1) % ways) for d in range(ways)])  16.1 us
    unnamed x22, local copies, waits for them, and re-layouts  10.9 us
    ppermute x8, waiting for transfers between devices, collect(): lax.ppermute(going_up, axis, [(d, (d + 1) % ways) for d in range(ways)])  3.97 us
  transfers between devices with their start and end apart: 18, of which 6 were waited for; matrix products, arithmetic and copies ran while one was open for 5% of the time, Pallas kernels for 0%

profile of v1, /device:TPU:0, one launch (start us, length us, event | category | flops | bytes accessed | tf_op | source)
XLA Modules:
  0.0 186.0 jit_solution(13667729301216434335)
XLA Ops:
  7.2 0.0 reduce-scatter.13.cloned.1.call-start
  7.2 0.8 slice_bitcast_fusion.1
  8.0 0.5 collective-permute-start
  8.5 2.9 %collective-permute-start.1 = (bf16[128,64]{0,1:T(8,128)(2,1)S(1)}, bf16[128,64]{0,1:T(8,128)(2,1)S(1)}, u32[]{:S(2)}, u32[]{:S(2)}) collective-permute-start(bf16[128,64]{0,1:T(8,128)(2,1)S(1)} %get-tuple-element.9), channel_id=1, source_target_pairs={{0,28},{4,0},{8,4},{12,8},{16,12},{20,16},{24,20},{28,24},{1,29},{... | collective-permute-start | bytes 49160 | tf_op jit(solution)/shard_map/ppermute | solution.py:19
  11.4 2.6 %collective-permute-start.8 = (bf16[128,64]{0,1:T(8,128)(2,1)S(1)}, bf16[128,64]{0,1:T(8,128)(2,1)S(1)}, u32[]{:S(2)}, u32[]{:S(2)}) collective-permute-start(bf16[128,64]{0,1:T(8,128)(2,1)S(1)} %get-tuple-element.10), channel_id=1, source_target_pairs={{0,28},{4,0},{8,4},{12,8},{16,12},{20,16},{24,20},{28,24},{1,29},{... | collective-permute-start | bytes 49160 | tf_op jit(solution)/shard_map/ppermute | solution.py:19
  14.1 0.7 copy-done.3
  14.9 0.7 copy-done.4
  15.5 2.6 %collective-permute-start.3 = (bf16[128,64]{0,1:T(8,128)(2,1)S(1)}, bf16[128,64]{0,1:T(8,128)(2,1)S(1)}, u32[]{:S(2)}, u32[]{:S(2)}) collective-permute-start(bf16[128,64]{0,1:T(8,128)(2,1)S(1)} %collective-permute-done.1), channel_id=1, source_target_pairs={{0,28},{4,0},{8,4},{12,8},{16,12},{20,16},{24,20},{28,24},{1,29},{... | collective-permute-start | bytes 49160 | tf_op jit(solution)/shard_map/ppermute | solution.py:19
  18.2 2.6 %collective-permute-start.10 = (bf16[128,64]{0,1:T(8,128)(2,1)S(1)}, bf16[128,64]{0,1:T(8,128)(2,1)S(1)}, u32[]{:S(2)}, u32[]{:S(2)}) collective-permute-start(bf16[128,64]{0,1:T(8,128)(2,1)S(1)} %collective-permute-done.8), channel_id=1, source_target_pairs={{0,28},{4,0},{8,4},{12,8},{16,12},{20,16},{24,20},{28,24},{1,29},{... | collective-permute-start | bytes 49160 | tf_op jit(solution)/shard_map/ppermute | solution.py:19
  20.9 0.1 collective-permute-start.4
  21.0 2.6 %collective-permute-start.5 = (bf16[128,64]{0,1:T(8,128)(2,1)S(1)}, bf16[128,64]{0,1:T(8,128)(2,1)S(1)}, u32[]{:S(2)}, u32[]{:S(2)}) collective-permute-start(bf16[128,64]{0,1:T(8,128)(2,1)S(1)} %collective-permute-done.3), channel_id=1, source_target_pairs={{0,28},{4,0},{8,4},{12,8},{16,12},{20,16},{24,20},{28,24},{1,29},{... | collective-permute-start | bytes 49160 | tf_op jit(solution)/shard_map/ppermute | solution.py:19
  23.6 2.6 %collective-permute-start.12 = (bf16[128,64]{0,1:T(8,128)(2,1)S(1)}, bf16[128,64]{0,1:T(8,128)(2,1)S(1)}, u32[]{:S(2)}, u32[]{:S(2)}) collective-permute-start(bf16[128,64]{0,1:T(8,128)(2,1)S(1)} %collective-permute-done.10), channel_id=1, source_target_pairs={{0,28},{4,0},{8,4},{12,8},{16,12},{20,16},{24,20},{28,24},{1,29},{... | collective-permute-start | bytes 49160 | tf_op jit(solution)/shard_map/ppermute | solution.py:19
  26.3 0.1 collective-permute-start.6
  26.4 1.3 collective-permute-done.11
  27.8 2.7 %collective-permute-done.6 = bf16[128,64]{0,1:T(8,128)(2,1)S(1)} collective-permute-done((bf16[128,64]{0,1:T(8,128)(2,1)S(1)}, bf16[128,64]{0,1:T(8,128)(2,1)S(1)}, u32[]{:S(2)}, u32[]{:S(2)}) %collective-permute-start.6) | collective-permute-done | bytes 16416 | tf_op jit(solution)/shard_map/ppermute | solution.py:16
  30.4 17.2 %all_gather.6 = bf16[1024,256]{0,1:T(8,128)(2,1)S(1)} all-gather(bf16[1024,64]{0,1:T(8,128)(2,1)S(1)} %constant_dynamic-update-slice_fusion.8), channel_id=1, replica_groups=mesh['wide'=8,'narrow'=4] {'narrow'}, dimensions={1}, use_global_device_ids=true | all-gather | bytes 655360 | tf_op jit(solution)/shard_map/all_gather | solution.py:37
  47.6 16.1 %all_gather.7 = bf16[1024,256]{0,1:T(8,128)(2,1)S(1)} all-gather(bf16[1024,64]{0,1:T(8,128)(2,1)S(1)} %constant_dynamic-update-slice_fusion), channel_id=1, replica_groups=mesh['wide'=8,'narrow'=4] {'narrow'}, dimensions={1}, use_global_device_ids=true | all-gather | bytes 655360 | tf_op jit(solution)/shard_map/all_gather | solution.py:37
  63.7 0.5 fusion.9
  64.2 0.7 copy-done.5
  64.9 0.5 fusion.7
  65.4 0.4 fusion.4
  65.9 1.0 copy.12
  66.9 0.0 reduce-scatter.13.cloned.1.call-update
  66.9 0.0 reduce-scatter.15.cloned.1.call-start
  67.0 0.5 fusion.10
  67.4 0.7 copy-done.6
  68.2 0.5 fusion.6
  68.7 0.7 copy-done.1
  69.4 0.4 fusion.5
  69.8 1.0 copy.14
  70.8 0.0 reduce-scatter.15.cloned.1.call-update
  70.9 0.0 reduce-scatter.9.cloned.1.call-start
  71.0 28.3 %reduce-scatter.13.cloned.1.call-done = bf16[128,256]{1,0:T(8,128)(2,1)} async-done(((bf16[1024,256]{1,0:T(8,128)(2,1)}), bf16[128,256]{1,0:T(8,128)(2,1)}) %reduce-scatter.13.cloned.1.call-update) | async-done | bytes 65552
  99.2 1.6 copy.13
  100.8 0.0 reduce-scatter.9.cloned.1.call-update
  100.8 0.0 reduce-scatter.11.cloned.1.call-start
  100.9 0.1 pad_maximum_fusion
  101.0 1.1 copy.10
  102.1 0.1 pad_maximum_fusion.1
  102.1 1.1 copy.11
  103.2 33.3 %reduce-scatter.15.cloned.1.call-done = bf16[128,256]{1,0:T(8,128)(2,1)} async-done(((bf16[1024,256]{1,0:T(8,128)(2,1)}), bf16[128,256]{1,0:T(8,128)(2,1)}) %reduce-scatter.15.cloned.1.call-update) | async-done | bytes 65552
  136.5 1.6 copy.15
  138.1 0.0 reduce-scatter.11.cloned.1.call-update
  138.1 20.0 %reduce-scatter.9.cloned.1.call-done = bf16[128,64]{0,1:T(8,128)(2,1)} async-done(((bf16[128,256]{0,1:T(8,128)(2,1)}), bf16[128,64]{0,1:T(8,128)(2,1)}) %reduce-scatter.9.cloned.1.call-update) | async-done | bytes 16400 | tf_op jit(solution)/shard_map/reduce_scatter | solution.py:51
  158.0 0.7 multiply_bitcast_fusion.1
  158.8 19.4 %reduce-scatter.11.cloned.1.call-done = bf16[128,64]{0,1:T(8,128)(2,1)} async-done(((bf16[128,256]{0,1:T(8,128)(2,1)}), bf16[128,64]{0,1:T(8,128)(2,1)}) %reduce-scatter.11.cloned.1.call-update) | async-done | bytes 16400 | tf_op jit(solution)/shard_map/reduce_scatter | solution.py:51
  178.1 0.7 multiply_bitcast_fusion
  178.9 0.6 pad_maximum_fusion.2
  (49 shorter events, 0.4 us)
Async XLA Ops:
  7.2 56.5 %copy-start = (bf16[512,1024]{1,0:T(8,128)(2,1)S(1)}, bf16[512,1024]{1,0:T(8,128)(2,1)}, u32[]{:S(2)}) copy-start(bf16[512,1024]{1,0:T(8,128)(2,1)} %param.5) | copy-start | bytes 3145732
  7.2 92.1 %reduce-scatter.13.cloned.1.call-start = ((), (), s32[]{:S(2)}) async-start(), calls=%async_computation.6 | async-start | bytes 589824
  8.0 7.5 %collective-permute-start = (bf16[128,64]{0,1:T(8,128)(2,1)S(1)}, bf16[128,64]{0,1:T(8,128)(2,1)S(1)}, u32[]{:S(2)}, u32[]{:S(2)}) collective-permute-start(bf16[128,64]{0,1:T(8,128)(2,1)S(1)} %get-tuple-element.9), channel_id=1, source_target_pairs={{0,4},{4,8},{8,12},{12,16},{16,20},{20,24},{24,28},{28,0},{1,5},{5... | collective-permute-start | bytes 49160 | tf_op jit(solution)/shard_map/ppermute | solution.py:16
  8.5 7.0 %collective-permute-start.1 = (bf16[128,64]{0,1:T(8,128)(2,1)S(1)}, bf16[128,64]{0,1:T(8,128)(2,1)S(1)}, u32[]{:S(2)}, u32[]{:S(2)}) collective-permute-start(bf16[128,64]{0,1:T(8,128)(2,1)S(1)} %get-tuple-element.9), channel_id=1, source_target_pairs={{0,28},{4,0},{8,4},{12,8},{16,12},{20,16},{24,20},{28,24},{1,29},{... | collective-permute-start | bytes 49160 | tf_op jit(solution)/shard_map/ppermute | solution.py:19
  11.4 6.8 %collective-permute-start.7 = (bf16[128,64]{0,1:T(8,128)(2,1)S(1)}, bf16[128,64]{0,1:T(8,128)(2,1)S(1)}, u32[]{:S(2)}, u32[]{:S(2)}) collective-permute-start(bf16[128,64]{0,1:T(8,128)(2,1)S(1)} %get-tuple-element.10), channel_id=1, source_target_pairs={{0,4},{4,8},{8,12},{12,16},{16,20},{20,24},{24,28},{28,0},{1,5},{5... | collective-permute-start | bytes 49160 | tf_op jit(solution)/shard_map/ppermute | solution.py:16
  11.4 6.8 %collective-permute-start.8 = (bf16[128,64]{0,1:T(8,128)(2,1)S(1)}, bf16[128,64]{0,1:T(8,128)(2,1)S(1)}, u32[]{:S(2)}, u32[]{:S(2)}) collective-permute-start(bf16[128,64]{0,1:T(8,128)(2,1)S(1)} %get-tuple-element.10), channel_id=1, source_target_pairs={{0,28},{4,0},{8,4},{12,8},{16,12},{20,16},{24,20},{28,24},{1,29},{... | collective-permute-start | bytes 49160 | tf_op jit(solution)/shard_map/ppermute | solution.py:19
  14.1 0.8 copy-start.3
  14.8 0.7 copy-start.4
  15.5 5.4 %collective-permute-start.2 = (bf16[128,64]{0,1:T(8,128)(2,1)S(1)}, bf16[128,64]{0,1:T(8,128)(2,1)S(1)}, u32[]{:S(2)}, u32[]{:S(2)}) collective-permute-start(bf16[128,64]{0,1:T(8,128)(2,1)S(1)} %collective-permute-done), channel_id=1, source_target_pairs={{0,4},{4,8},{8,12},{12,16},{16,20},{20,24},{24,28},{28,0},{1,5},{5... | collective-permute-start | bytes 49160 | tf_op jit(solution)/shard_map/ppermute | solution.py:16
  15.5 5.4 %collective-permute-start.3 = (bf16[128,64]{0,1:T(8,128)(2,1)S(1)}, bf16[128,64]{0,1:T(8,128)(2,1)S(1)}, u32[]{:S(2)}, u32[]{:S(2)}) collective-permute-start(bf16[128,64]{0,1:T(8,128)(2,1)S(1)} %collective-permute-done.1), channel_id=1, source_target_pairs={{0,28},{4,0},{8,4},{12,8},{16,12},{20,16},{24,20},{28,24},{1,29},{... | collective-permute-start | bytes 49160 | tf_op jit(solution)/shard_map/ppermute | solution.py:19
  18.2 5.4 %collective-permute-start.9 = (bf16[128,64]{0,1:T(8,128)(2,1)S(1)}, bf16[128,64]{0,1:T(8,128)(2,1)S(1)}, u32[]{:S(2)}, u32[]{:S(2)}) collective-permute-start(bf16[128,64]{0,1:T(8,128)(2,1)S(1)} %collective-permute-done.7), channel_id=1, source_target_pairs={{0,4},{4,8},{8,12},{12,16},{16,20},{20,24},{24,28},{28,0},{1,5},{5... | collective-permute-start | bytes 49160 | tf_op jit(solution)/shard_map/ppermute | solution.py:16
  18.2 5.4 %collective-permute-start.10 = (bf16[128,64]{0,1:T(8,128)(2,1)S(1)}, bf16[128,64]{0,1:T(8,128)(2,1)S(1)}, u32[]{:S(2)}, u32[]{:S(2)}) collective-permute-start(bf16[128,64]{0,1:T(8,128)(2,1)S(1)} %collective-permute-done.8), channel_id=1, source_target_pairs={{0,28},{4,0},{8,4},{12,8},{16,12},{20,16},{24,20},{28,24},{1,29},{... | collective-permute-start | bytes 49160 | tf_op jit(solution)/shard_map/ppermute | solution.py:19
  20.9 5.4 %collective-permute-start.4 = (bf16[128,64]{0,1:T(8,128)(2,1)S(1)}, bf16[128,64]{0,1:T(8,128)(2,1)S(1)}, u32[]{:S(2)}, u32[]{:S(2)}) collective-permute-start(bf16[128,64]{0,1:T(8,128)(2,1)S(1)} %collective-permute-done.2), channel_id=1, source_target_pairs={{0,4},{4,8},{8,12},{12,16},{16,20},{20,24},{24,28},{28,0},{1,5},{5... | collective-permute-start | bytes 49160 | tf_op jit(solution)/shard_map/ppermute | solution.py:16
  21.0 6.8 %collective-permute-start.5 = (bf16[128,64]{0,1:T(8,128)(2,1)S(1)}, bf16[128,64]{0,1:T(8,128)(2,1)S(1)}, u32[]{:S(2)}, u32[]{:S(2)}) collective-permute-start(bf16[128,64]{0,1:T(8,128)(2,1)S(1)} %collective-permute-done.3), channel_id=1, source_target_pairs={{0,28},{4,0},{8,4},{12,8},{16,12},{20,16},{24,20},{28,24},{1,29},{... | collective-permute-start | bytes 49160 | tf_op jit(solution)/shard_map/ppermute | solution.py:19
  23.6 4.1 %collective-permute-start.11 = (bf16[128,64]{0,1:T(8,128)(2,1)S(1)}, bf16[128,64]{0,1:T(8,128)(2,1)S(1)}, u32[]{:S(2)}, u32[]{:S(2)}) collective-permute-start(bf16[128,64]{0,1:T(8,128)(2,1)S(1)} %collective-permute-done.9), channel_id=1, source_target_pairs={{0,4},{4,8},{8,12},{12,16},{16,20},{20,24},{24,28},{28,0},{1,5},{5... | collective-permute-start | bytes 49160 | tf_op jit(solution)/shard_map/ppermute | solution.py:16
  23.6 4.1 %collective-permute-start.12 = (bf16[128,64]{0,1:T(8,128)(2,1)S(1)}, bf16[128,64]{0,1:T(8,128)(2,1)S(1)}, u32[]{:S(2)}, u32[]{:S(2)}) collective-permute-start(bf16[128,64]{0,1:T(8,128)(2,1)S(1)} %collective-permute-done.10), channel_id=1, source_target_pairs={{0,28},{4,0},{8,4},{12,8},{16,12},{20,16},{24,20},{28,24},{1,29},{... | collective-permute-start | bytes 49160 | tf_op jit(solution)/shard_map/ppermute | solution.py:19
  26.3 4.1 %collective-permute-start.6 = (bf16[128,64]{0,1:T(8,128)(2,1)S(1)}, bf16[128,64]{0,1:T(8,128)(2,1)S(1)}, u32[]{:S(2)}, u32[]{:S(2)}) collective-permute-start(bf16[128,64]{0,1:T(8,128)(2,1)S(1)} %collective-permute-done.4), channel_id=1, source_target_pairs={{0,4},{4,8},{8,12},{12,16},{16,20},{20,24},{24,28},{28,0},{1,5},{5... | collective-permute-start | bytes 49160 | tf_op jit(solution)/shard_map/ppermute | solution.py:16
  27.7 19.9 %collective-permute-start.13 = (bf16[128,64]{0,1:T(8,128)(2,1)S(1)}, bf16[128,64]{0,1:T(8,128)(2,1)S(1)}, u32[]{:S(2)}, u32[]{:S(2)}) collective-permute-start(bf16[128,64]{0,1:T(8,128)(2,1)S(1)} %collective-permute-done.11), channel_id=1, source_target_pairs={{0,4},{4,8},{8,12},{12,16},{16,20},{20,24},{24,28},{28,0},{1,5},{5... | collective-permute-start | bytes 49160 | tf_op jit(solution)/shard_map/ppermute | solution.py:16
  63.7 1.2 copy-start.5
  64.2 0.7 copy-start.7
  66.9 69.6 %reduce-scatter.15.cloned.1.call-start = ((), (), s32[]{:S(2)}) async-start(), calls=%async_computation.7 | async-start | bytes 589824
  66.9 1.2 copy-start.6
  68.7 0.7 copy-start.1
  70.9 87.2 %reduce-scatter.9.cloned.1.call-start = ((), (), s32[]{:S(2)}) async-start(), calls=%async_computation.4 | async-start | bytes 81920 | tf_op jit(solution)/shard_map/reduce_scatter | solution.py:51
  100.8 77.3 %reduce-scatter.11.cloned.1.call-start = ((), (), s32[]{:S(2)}) async-start(), calls=%async_computation.5 | async-start | bytes 81920 | tf_op jit(solution)/shard_map/reduce_scatter | solution.py:51
  100.9 1.1 copy-start.2
Sparse Core Ops, SparseCore 0:
  67.0 32.1 reduce-scatter.12
  102.3 34.1 reduce-scatter.14
  138.7 19.2 reduce-scatter.8
  160.7 17.3 reduce-scatter.10
